TPU v7x, 32 devices: a whole 2x2x4 slice. The times are simulated.
32 devices in a mesh: hid: 8 (over y, x, core), tok: 4 (over z).
Axes of the slice: x: 2, y: 2, z: 4, core: 2. Of those that a mesh axis runs over, the one named last changes fastest.
Arguments:
- tokens: bfloat16 [896, 8192], P('tok', 'hid'), may hold values from -6 to 6
- in_blocks: bfloat16 [128, 6, 256, 256], P('hid', None, 'tok'), may hold values from -0.15625 to 0.15625
- in_left: bfloat16 [8192, 256], P(('hid', 'tok')), may hold values from -0.0625 to 0.0625
- in_right: bfloat16 [256, 32768], P(None, ('hid', 'tok')), may hold values from -0.375 to 0.375
- in_lists: int32 [128, 6], replicated, may hold values from 0 to 31, as said below
- out_blocks: bfloat16 [128, 6, 256, 256], P('hid', None, 'tok'), may hold values from -0.078125 to 0.078125
- out_left: bfloat16 [32768, 256], P(('hid', 'tok')), may hold values from -0.03125 to 0.03125
- out_right: bfloat16 [256, 8192], P(None, ('hid', 'tok')), may hold values from -0.375 to 0.375
- out_lists: int32 [128, 6], replicated, may hold values from 0 to 31, as said below
- cotangent: bfloat16 [896, 8192], P('tok', 'hid'), may hold values from -6 to 6
Outputs:
- layer_out: bfloat16 [896, 8192], P('tok', 'hid')
- grad_tokens: bfloat16 [896, 8192], P('tok', 'hid')
- grad_in_blocks: bfloat16 [128, 6, 256, 256], P('hid', None, 'tok')
- grad_in_left: bfloat16 [8192, 256], P(('hid', 'tok'))
- grad_in_right: bfloat16 [256, 32768], P(None, ('hid', 'tok'))
- grad_out_blocks: bfloat16 [128, 6, 256, 256], P('hid', None, 'tok')
- grad_out_left: bfloat16 [32768, 256], P(('hid', 'tok'))
- grad_out_right: bfloat16 [256, 8192], P(None, ('hid', 'tok'))
Inputs may be any that keep to these rules, and one draw needn't show every extreme that they name: There is one whole number m, the same for every row, with in_lists[c, 0] = ((c * 8192) // 32768) XOR m, and in_lists[c, k] = in_lists[c, 0] XOR 2^(k-1) for k = 1 to 5. `out_lists`: the same butterfly form as in_lists, with its own number m, which differs from that of in_lists.
All inputs are finite; a program needn't handle non-finite values.
Results may differ from a plain program's by a relative error of at most 0.012.
Values may be sent and summed in bfloat16 or wider, within the bound.
A program may use at most 256 MiB of HBM per device.

v0:
```python
import jax
import jax.numpy as jnp
from jax import lax
from jax.sharding import PartitionSpec as P

D = 8192
BLK = 256


def gelu_parts(preact):
    inner_coef = 0.7978845608028654
    cubic_coef = 0.044715
    inner_arg = inner_coef * (preact + cubic_coef * preact * preact * preact)
    tanh_val = jnp.tanh(inner_arg)
    active = 0.5 * preact * (1.0 + tanh_val)
    slopes = 0.5 * (1.0 + tanh_val) + 0.5 * preact * (1.0 - tanh_val * tanh_val) * inner_coef * (
        1.0 + 3.0 * cubic_coef * preact * preact
    )
    return (active, slopes)


def dot_rows(left_arr, right_arr):
    return lax.dot_general(
        left_arr, right_arr, (((0,), (0,)), ((), ())), preferred_element_type=jnp.float32
    )


def dot_cols(left_arr, right_arr):
    return lax.dot_general(
        left_arr, right_arr, (((1,), (1,)), ((), ())), preferred_element_type=jnp.float32
    )


def rank_sum(values):
    return lax.psum(values, "hid")


def own_lists(lists, hid_blocks):
    return lax.dynamic_slice_in_dim(lists, lax.axis_index("hid") * hid_blocks, hid_blocks, 0)


def gather_in(values, lists, hid_blocks, blk_width):
    whole = lax.all_gather(values, "hid", axis=1, tiled=True)
    mine = own_lists(lists, hid_blocks)
    blocks = whole.reshape(whole.shape[0], whole.shape[1] // blk_width, blk_width)
    return blocks[:, mine.T]


def scatter_out(parts, lists, hid_blocks):
    mine = own_lists(lists, hid_blocks)
    picker = (mine.T[:, :, None] == jnp.arange(D // BLK, dtype=jnp.int32)[None, None, :]).astype(
        jnp.float32
    )
    dense = jnp.einsum("nsho,shc->nco", parts, picker, precision=lax.Precision.HIGHEST)
    return lax.psum_scatter(
        dense.reshape(dense.shape[0], -1), "hid", scatter_dimension=1, tiled=True
    )


def route_in(values, lists, hid_blocks, blk_width):
    return gather_in(values, lists, hid_blocks, blk_width)


def route_out(parts, lists, hid_blocks):
    return scatter_out(parts, lists, hid_blocks)


def local(
    tokens,
    in_blocks,
    in_left,
    in_right,
    in_lists,
    out_blocks,
    out_left,
    out_right,
    out_lists,
    cotangent,
):
    row_count, col_span = tokens.shape
    hid_blocks = in_blocks.shape[0]
    slot_count = in_blocks.shape[1]
    blk_width = in_blocks.shape[3]
    tok_count = lax.axis_size("tok")
    w_first, w_second, left_one, right_one, left_two, right_two = (
        lax.all_gather(in_blocks, "tok", axis=2, tiled=True),
        lax.all_gather(out_blocks, "tok", axis=2, tiled=True),
        lax.all_gather(in_left, "tok", axis=0, tiled=True),
        lax.all_gather(in_right, "tok", axis=1, tiled=True),
        lax.all_gather(out_left, "tok", axis=0, tiled=True),
        lax.all_gather(out_right, "tok", axis=1, tiled=True),
    )
    low_in, low_back = rank_sum(
        (
            jnp.dot(tokens, left_one, preferred_element_type=jnp.float32),
            dot_cols(cotangent, right_two),
        )
    )
    low_in = low_in.astype(jnp.bfloat16)
    low_back = low_back.astype(jnp.bfloat16)
    gathered = route_in(tokens, in_lists, hid_blocks, blk_width)
    group_count = gathered.shape[2]
    per_group = hid_blocks // group_count
    first_r = w_first.reshape(group_count, per_group, slot_count, blk_width, blk_width)
    second_r = w_second.reshape(group_count, per_group, slot_count, blk_width, blk_width)
    preact = jnp.einsum(
        "nseb,eqsbf->neqf", gathered, first_r, preferred_element_type=jnp.float32
    ).reshape(row_count, -1)
    preact = preact + jnp.dot(low_in, right_one, preferred_element_type=jnp.float32)
    active, slopes = gelu_parts(preact)
    hidden = active.astype(jnp.bfloat16)
    low_mid = rank_sum(jnp.dot(hidden, left_two, preferred_element_type=jnp.float32)).astype(
        jnp.bfloat16
    )
    hidden_r = hidden.reshape(row_count, group_count, per_group, blk_width)
    out_parts = jnp.einsum(
        "neqf,eqsfo->nseo", hidden_r, second_r, preferred_element_type=jnp.float32
    )
    sparse_out = route_out(out_parts, out_lists, hid_blocks)
    layer_out = (
        sparse_out + jnp.dot(low_mid, right_two, preferred_element_type=jnp.float32)
    ).astype(jnp.bfloat16)
    grad_in = route_in(cotangent, out_lists, hid_blocks, blk_width)
    grad_hidden = jnp.einsum(
        "nseo,eqsfo->neqf", grad_in, second_r, preferred_element_type=jnp.float32
    ).reshape(row_count, -1)
    grad_hidden = grad_hidden + dot_cols(low_back, left_two)
    grad_pre = (grad_hidden * slopes).astype(jnp.bfloat16)
    low_grad = rank_sum(dot_cols(grad_pre, right_one)).astype(jnp.bfloat16)
    grad_pre_r = grad_pre.reshape(row_count, group_count, per_group, blk_width)
    back_parts = jnp.einsum(
        "neqf,eqsbf->nseb", grad_pre_r, first_r, preferred_element_type=jnp.float32
    )
    sparse_back = route_out(back_parts, in_lists, hid_blocks)
    grad_tokens = (sparse_back + dot_cols(low_grad, left_one)).astype(jnp.bfloat16)
    loss_scale = lax.rsqrt(jnp.float32(row_count * tok_count))
    terms = (
        loss_scale
        * jnp.einsum(
            "nseb,neqf->eqsbf", gathered, grad_pre_r, preferred_element_type=jnp.float32
        ).reshape(w_first.shape),
        loss_scale
        * jnp.einsum(
            "neqf,nseo->eqsfo", hidden_r, grad_in, preferred_element_type=jnp.float32
        ).reshape(w_second.shape),
        loss_scale * dot_rows(tokens, low_grad),
        loss_scale * dot_rows(low_in, grad_pre),
        loss_scale * dot_rows(hidden, low_back),
        loss_scale * dot_rows(low_mid, cotangent),
    )
    shares = (
        lax.psum_scatter(
            terms[0].astype(jnp.bfloat16), "tok", scatter_dimension=2, tiled=True
        ).astype(jnp.float32),
        lax.psum_scatter(
            terms[1].astype(jnp.bfloat16), "tok", scatter_dimension=2, tiled=True
        ).astype(jnp.float32),
        lax.psum_scatter(
            terms[2].astype(jnp.bfloat16), "tok", scatter_dimension=0, tiled=True
        ).astype(jnp.float32),
        lax.psum_scatter(
            terms[3].astype(jnp.bfloat16), "tok", scatter_dimension=1, tiled=True
        ).astype(jnp.float32),
        lax.psum_scatter(
            terms[4].astype(jnp.bfloat16), "tok", scatter_dimension=0, tiled=True
        ).astype(jnp.float32),
        lax.psum_scatter(
            terms[5].astype(jnp.bfloat16), "tok", scatter_dimension=1, tiled=True
        ).astype(jnp.float32),
    )
    return (
        layer_out,
        grad_tokens,
        shares[0].astype(jnp.bfloat16),
        shares[2].astype(jnp.bfloat16),
        shares[3].astype(jnp.bfloat16),
        shares[1].astype(jnp.bfloat16),
        shares[4].astype(jnp.bfloat16),
        shares[5].astype(jnp.bfloat16),
    )


def solution(mesh):
    return jax.shard_map(
        local,
        mesh=mesh,
        in_specs=(
            P("tok", "hid"),
            P("hid", None, "tok", None),
            P(("hid", "tok"), None),
            P(None, ("hid", "tok")),
            P(),
            P("hid", None, "tok", None),
            P(("hid", "tok"), None),
            P(None, ("hid", "tok")),
            P(),
            P("tok", "hid"),
        ),
        out_specs=(
            P("tok", "hid"),
            P("tok", "hid"),
            P("hid", None, "tok", None),
            P(("hid", "tok"), None),
            P(None, ("hid", "tok")),
            P("hid", None, "tok", None),
            P(("hid", "tok"), None),
            P(None, ("hid", "tok")),
        ),
        check_vma=False,
    )
```

profile of v0, /device:TPU:11, one launch (start us, length us, event | category | flops | bytes accessed | tf_op | source)
XLA Modules:
  0.0 1393.0 jit_solution(3682937672715421164)
XLA Ops:
  7.2 0.7 all-gather.7.cloned.1.call-update
  8.0 0.7 all-gather.17.cloned.1.call-update
  8.7 0.7 all-gather.13.cloned.1.call-update
  9.5 1.9 copy.54
  11.4 0.5 all-gather.11.cloned.1.call-update
  12.0 0.5 all-gather.15.cloned.1.call-update
  12.7 0.1 reshape.88
  12.8 0.1 compare_select_fusion
  12.9 0.1 reshape.96
  13.0 13.0 all_gather.26
  25.9 0.8 copy-done.5
  26.7 0.3 fusion.60
  27.1 13.2 all_gather.30
  40.3 0.8 copy-done.3
  41.1 0.3 fusion.62
  41.5 37.0 %all-reduce.4 = (bf16[224,256]{1,0:T(8,128)(2,1)S(1)}, bf16[224,256]{1,0:T(8,128)(2,1)S(1)}) all-reduce(f32[224,256]{1,0:T(8,128)S(1)} %fusion.60, f32[224,256]{1,0:T(8,128)S(1)} %fusion.62), channel_id=1, replica_groups=mesh['hid'=8,'tok'=4] {'hid'}, use_global_device_ids=true, to_apply=%region_0.0 | all-reduce | flops 114688 | bytes 688128 | tf_op jit(solution)/shard_map/psum | solution.py:35
  78.6 4.4 copy.130
  83.0 2.1 all-gather.17.cloned.1.call-done
  85.1 4.3 copy.129
  89.4 11.1 gather_fusion.1
  100.5 10.5 gather_fusion
  111.0 191.0 %all-gather.13.cloned.1.call-done = bf16[16,6,256,256]{3,2,1,0:T(8,128)(2,1)} async-done(((bf16[16,6,64,256]{3,2,1,0:T(8,128)(2,1)}), bf16[16,6,256,256]{3,2,1,0:T(8,128)(2,1)}) %all-gather.13.cloned.1.call-update) | async-done | bytes 12582928 | tf_op jit(solution)/shard_map/all_gather | solution.py:87
  301.9 9.8 fusion.57
  311.7 2.2 copy.92
  314.0 206.4 %all-gather.9.cloned.1.call-done = bf16[16,6,256,256]{3,2,0,1:T(8,128)(2,1)} async-done(((bf16[16,6,64,256]{3,2,0,1:T(8,128)(2,1)}), bf16[16,6,256,256]{3,2,0,1:T(8,128)(2,1)}) %all-gather.9.cloned.1.call-update) | async-done | bytes 12582928 | tf_op jit(solution)/shard_map/all_gather | solution.py:86
  520.4 12.0 fusion.56
  532.4 2.4 copy.89
  534.8 32.0 %all-gather.11.cloned.1.call-done = bf16[256,4096]{1,0:T(8,128)(2,1)} async-done(((bf16[256,1024]{1,0:T(8,128)(2,1)}), bf16[256,4096]{1,0:T(8,128)(2,1)}) %all-gather.11.cloned.1.call-update) | async-done | bytes 2097168 | tf_op jit(solution)/shard_map/all_gather | solution.py:89
  566.8 6.7 multiply_convert_fusion.2
  573.5 39.4 %all-gather.15.cloned.1.call-done = bf16[4096,256]{1,0:T(8,128)(2,1)} async-done(((bf16[1024,256]{1,0:T(8,128)(2,1)}), bf16[4096,256]{1,0:T(8,128)(2,1)}) %all-gather.15.cloned.1.call-update) | async-done | bytes 2097168 | tf_op jit(solution)/shard_map/all_gather | solution.py:90
  613.0 6.0 fusion.24
  619.0 0.9 fusion.63
  619.9 0.6 copy-done
  620.5 0.6 copy-done.11
  621.1 0.6 fusion.61
  621.8 28.2 %all-reduce.5 = (bf16[224,256]{1,0:T(8,128)(2,1)S(1)}, bf16[224,256]{1,0:T(8,128)(2,1)S(1)}) all-reduce(f32[224,256]{1,0:T(8,128)S(1)} %fusion.61, f32[224,256]{1,0:T(8,128)S(1)} %fusion.63), channel_id=1, replica_groups=mesh['hid'=8,'tok'=4] {'hid'}, use_global_device_ids=true, to_apply=%region_2.0 | all-reduce | flops 114688 | bytes 688128 | tf_op jit(solution)/shard_map/psum | solution.py:35
  649.9 1.2 fusion.41
  651.2 1.7 copy.93
  652.9 13.1 fusion.14
  666.0 28.7 %fusion = f32[32,224,256,1]{2,0,3,1:T(8,128)S(1)} fusion(f32[224,6,16,256]{3,0,1,2:T(8,128)} %fusion.14, s32[6,16]{1,0:T(8,128)S(1)} %get-tuple-element.47), kind=kOutput, calls=%fused_computation.4 | convolution fusion | flops 2113932288 | bytes 29360512 | tf_op jit(solution)/shard_map/nsho,shc->nco/dot_general | solution.py:54
  694.8 9.4 copy.94
  704.2 2.0 copy.90
  706.2 17.1 %convolution_bitcast_fusion = f32[224,6,16,256]{3,0,1,2:T(8,128)} fusion(bf16[16,6,256,256]{3,2,1,0:T(8,128)(2,1)} %all-gather.13.cloned.1.call-done, bf16[224,16,256,1]{2,1,0,3:T(8,128)(2,1)S(1)} %bitcast.141), kind=kOutput, calls=%fused_computation.19 | convolution fusion | flops 2818572288 | bytes 36438016 | tf_op jit(solution)/shard_map/neqf,eqsfo->nseo/dot_general | solution.py:116
  723.3 28.5 %fusion.2 = f32[32,224,256,1]{2,0,3,1:T(8,128)S(1)} fusion(f32[224,6,16,256]{3,0,1,2:T(8,128)} %convolution_bitcast_fusion, s32[6,16]{1,0:T(8,128)S(1)} %get-tuple-element.45), kind=kOutput, calls=%fused_computation.6 | convolution fusion | flops 2113932288 | bytes 29360512 | tf_op jit(solution)/shard_map/nsho,shc->nco/dot_general | solution.py:54
  751.8 9.5 copy.91
  761.4 11.4 fusion.5
  772.9 17.8 %copy.69 = bf16[16,6,256,256]{3,0,1,2:T(8,128)(2,1)} copy(bf16[16,6,256,256]{2,3,1,0:T(8,128)(2,1)} %fusion.5) | data formatting | bytes 25165824 | tf_op jit(solution)/shard_map/convert_element_type | solution.py:156
  790.8 12.6 fusion.4
  803.3 16.8 %copy.66 = bf16[16,6,256,256]{3,0,1,2:T(8,128)(2,1)} copy(bf16[16,6,256,256]{2,3,1,0:T(8,128)(2,1)} %fusion.4) | data formatting | bytes 25165824 | tf_op jit(solution)/shard_map/convert_element_type | solution.py:153
  820.2 0.9 copy-done.9
  821.1 1.1 fusion.38
  822.3 3.7 fusion.23
  826.1 2.0 fusion.22
  828.2 1.7 copy.71
  829.9 2.3 fusion.40
  832.2 10.3 reduce-scatter.9.cloned.1.call-done
  842.5 2.2 fusion.39
  844.7 212.0 %reduce-scatter.19.cloned.1.call-done = bf16[16,6,64,256]{3,0,1,2:T(8,128)(2,1)} async-done(((bf16[16,6,256,256]{3,0,1,2:T(8,128)(2,1)}), bf16[16,6,64,256]{3,0,1,2:T(8,128)(2,1)}) %reduce-scatter.19.cloned.1.call-update) | async-done | bytes 3145744 | tf_op jit(solution)/shard_map/reduce_scatter | solution.py:155
  1056.7 5.3 copy.72
  1062.0 209.9 %reduce-scatter.13.cloned.1.call-done = bf16[16,6,64,256]{3,0,1,2:T(8,128)(2,1)} async-done(((bf16[16,6,256,256]{3,0,1,2:T(8,128)(2,1)}), bf16[16,6,64,256]{3,0,1,2:T(8,128)(2,1)}) %reduce-scatter.13.cloned.1.call-update) | async-done | bytes 3145744 | tf_op jit(solution)/shard_map/reduce_scatter | solution.py:152
  1271.9 5.3 copy.70
  1277.3 16.2 %reduce-scatter.23.cloned.1.call-done = bf16[256,256]{1,0:T(8,128)(2,1)} async-done(((bf16[256,1024]{1,0:T(8,128)(2,1)}), bf16[256,256]{1,0:T(8,128)(2,1)}) %reduce-scatter.23.cloned.1.call-update) | async-done | bytes 131088 | tf_op jit(solution)/shard_map/reduce_scatter | solution.py:167
  1293.5 46.5 %reduce-scatter.21.cloned.1.call-done = bf16[1024,256]{1,0:T(8,128)(2,1)} async-done(((bf16[4096,256]{1,0:T(8,128)(2,1)}), bf16[1024,256]{1,0:T(8,128)(2,1)}) %reduce-scatter.21.cloned.1.call-update) | async-done | bytes 524304 | tf_op jit(solution)/shard_map/reduce_scatter | solution.py:164
  1339.9 46.1 %reduce-scatter.17.cloned.1.call-done = bf16[256,1024]{1,0:T(8,128)(2,1)} async-done(((bf16[256,4096]{1,0:T(8,128)(2,1)}), bf16[256,1024]{1,0:T(8,128)(2,1)}) %reduce-scatter.17.cloned.1.call-update) | async-done | bytes 524304 | tf_op jit(solution)/shard_map/reduce_scatter | solution.py:161
  (56 shorter events, 0.9 us)
Async XLA Ops:
  7.2 2.3 copy-start.10
  7.2 71.4 %all-gather.7.cloned.1.call-start = ((), (), s32[]{:S(2)}) async-start(), calls=%async_computation.8 | async-start | bytes 4128768 | tf_op jit(solution)/shard_map/all_gather | solution.py:43
  7.9 77.2 %all-gather.17.cloned.1.call-start = ((), (), s32[]{:S(2)}) async-start(), calls=%async_computation.14 | async-start | bytes 4128768 | tf_op jit(solution)/shard_map/all_gather | solution.py:43
  8.7 293.3 %all-gather.13.cloned.1.call-start = ((), (), s32[]{:S(2)}) async-start(), calls=%async_computation.11 | async-start | bytes 15728640 | tf_op jit(solution)/shard_map/all_gather | solution.py:87
  9.4 511.0 %all-gather.9.cloned.1.call-start = ((), (), s32[]{:S(2)}) async-start(), calls=%async_computation.9 | async-start | bytes 15728640 | tf_op jit(solution)/shard_map/all_gather | solution.py:86
  11.3 1.3 copy-start.14
  11.3 1.5 copy-start.15
  11.3 1.6 copy-start.12
  11.3 15.4 %copy-start.7 = (bf16[224,1024]{1,0:T(8,128)(2,1)S(1)}, bf16[224,1024]{1,0:T(8,128)(2,1)}, u32[]{:S(2)}) copy-start(bf16[224,1024]{1,0:T(8,128)(2,1)} %param.10) | copy-start | bytes 1376260
  11.3 15.7 %copy-start.13 = (bf16[256,256]{1,0:T(8,128)(2,1)S(1)}, bf16[256,256]{1,0:T(8,128)(2,1)}, u32[]{:S(2)}) copy-start(bf16[256,256]{1,0:T(8,128)(2,1)} %param.17) | copy-start | bytes 393220
  11.4 29.8 %copy-start.8 = (bf16[224,1024]{1,0:T(8,128)(2,1)S(1)}, bf16[224,1024]{1,0:T(8,128)(2,1)}, u32[]{:S(2)}) copy-start(bf16[224,1024]{1,0:T(8,128)(2,1)} %param.19) | copy-start | bytes 1376260
  11.4 555.4 %all-gather.11.cloned.1.call-start = ((), (), s32[]{:S(2)}) async-start(), calls=%async_computation.10 | async-start | bytes 2621440 | tf_op jit(solution)/shard_map/all_gather | solution.py:89
  12.0 601.0 %all-gather.15.cloned.1.call-start = ((), (), s32[]{:S(2)}) async-start(), calls=%async_computation.13 | async-start | bytes 2621440 | tf_op jit(solution)/shard_map/all_gather | solution.py:90
  12.6 815.6 %reduce-scatter.15.cloned.1.call-start = ((), (), s32[]{:S(2)}) async-start(), calls=%async_computation.17 | async-start | bytes 655360 | tf_op jit(solution)/shard_map/reduce_scatter | solution.py:158
  25.9 0.8 copy-start.5
  40.3 0.8 copy-start.3
  613.0 6.0 copy-start.2
  619.0 1.5 copy-start
  619.0 2.1 copy-start.11
  651.1 178.7 %reduce-scatter.11.cloned.1.call-start = ((), (), s32[]{:S(2)}) async-start(), calls=%async_computation.15 | async-start | bytes 8257536 | tf_op jit(solution)/shard_map/reduce_scatter | solution.py:55
  704.2 138.3 %reduce-scatter.9.cloned.1.call-start = ((), (), s32[]{:S(2)}) async-start(), calls=%async_computation.12 | async-start | bytes 8257536 | tf_op jit(solution)/shard_map/reduce_scatter | solution.py:55
  706.2 17.1 %copy-start.1 = (bf16[28,8,16,256]{3,2,1,0:T(8,128)(2,1)}, bf16[28,8,16,256]{3,2,1,0:T(8,128)(2,1)S(1)}, u32[]{:S(2)}) copy-start(bf16[28,8,16,256]{3,2,1,0:T(8,128)(2,1)S(1)} %copy.90) | copy-start | bytes 5505028
  761.4 295.3 %reduce-scatter.19.cloned.1.call-start = ((), (), s32[]{:S(2)}) async-start(), calls=%async_computation.19 | async-start | bytes 15728640 | tf_op jit(solution)/shard_map/reduce_scatter | solution.py:155
  790.7 481.2 %reduce-scatter.13.cloned.1.call-start = ((), (), s32[]{:S(2)}) async-start(), calls=%async_computation.16 | async-start | bytes 15728640 | tf_op jit(solution)/shard_map/reduce_scatter | solution.py:152
  820.1 1.0 copy-start.9
  820.1 473.3 %reduce-scatter.23.cloned.1.call-start = ((), (), s32[]{:S(2)}) async-start(), calls=%async_computation.21 | async-start | bytes 655360 | tf_op jit(solution)/shard_map/reduce_scatter | solution.py:167
  822.3 517.7 %reduce-scatter.21.cloned.1.call-start = ((), (), s32[]{:S(2)}) async-start(), calls=%async_computation.20 | async-start | bytes 2621440 | tf_op jit(solution)/shard_map/reduce_scatter | solution.py:164
  826.0 3.8 copy-start.6
  826.0 16.4 %copy-start.4 = (bf16[256,1024]{1,0:T(8,128)(2,1)S(1)}, bf16[256,1024]{1,0:T(8,128)(2,1)}, u32[]{:S(2)}) copy-start(bf16[256,1024]{1,0:T(8,128)(2,1)} %copy-done.3) | copy-start | bytes 1572868
  826.1 559.9 %reduce-scatter.17.cloned.1.call-start = ((), (), s32[]{:S(2)}) async-start(), calls=%async_computation.18 | async-start | bytes 2621440 | tf_op jit(solution)/shard_map/reduce_scatter | solution.py:161
Sparse Core Ops, SparseCore 0:
  9.9 36.0 all-gather.6
  47.9 37.1 all-gather.16
  86.7 215.2 all-gather.12
  303.9 216.3 all-gather.8
  521.8 45.0 all-gather.10
  568.3 44.6 all-gather.14
  651.3 18.3 reduce-scatter.14
  704.3 67.4 reduce-scatter.10
  775.5 66.9 reduce-scatter.8
  844.7 211.9 reduce-scatter.18
  1059.0 212.8 reduce-scatter.12
  1274.6 18.7 reduce-scatter.22
  1296.3 43.5 reduce-scatter.20
  1342.8 43.1 reduce-scatter.16
where the time goes:
time: 1410 us; the launch traced here: 1390 us
  waiting for transfers between devices  1020 us (72%)
  matrix products  161 us (11%)
  local copies, waits for them, and re-layouts  110 us (8%)
  blocking collectives  91.4 us (6%)
  between operations  14.6 us (1%)
    reduce_scatter x1, waiting for transfers between devices, local(): lax.psum_scatter(terms[1].astype(jnp.bfloat16), 'tok', scatter_dimension=...  212 us
    reduce_scatter x1, waiting for transfers between devices, local(): lax.psum_scatter(terms[0].astype(jnp.bfloat16), 'tok', scatter_dimension=...  210 us
    all_gather x1, waiting for transfers between devices, local(): lax.all_gather(in_blocks, 'tok', axis=2, tiled=True)  206 us
    all_gather x1, waiting for transfers between devices, local(): lax.all_gather(out_blocks, 'tok', axis=2, tiled=True)  191 us
    psum x2, blocking collectives, rank_sum(): return lax.psum(values, 'hid')  65.2 us
    dot_general x2, matrix products, scatter_out(): jnp.einsum('nsho,shc->nco', parts, picker, precision=lax.Precision.HIGHEST)  57.2 us
    reduce_scatter x1, waiting for transfers between devices, local(): lax.psum_scatter(terms[4].astype(jnp.bfloat16), 'tok', scatter_dimension=...  46.5 us
    reduce_scatter x1, waiting for transfers between devices, local(): lax.psum_scatter(terms[3].astype(jnp.bfloat16), 'tok', scatter_dimension=...  46.1 us
  transfers between devices with their start and end apart: 14, of which 11 were waited for; matrix products, arithmetic and copies ran while one was open for 19% of the time, Pallas kernels for 0%

commit v1 on v0

--- a/solution.py
+++ b/solution.py
@@ -65,7 +65,7 @@
     return scatter_out(parts, lists, hid_blocks)
 
 
-def local(
+def local_gathered(
     tokens,
     in_blocks,
     in_left,
@@ -178,6 +178,282 @@
         shares[4].astype(jnp.bfloat16),
         shares[5].astype(jnp.bfloat16),
     )
+
+
+def swap_tok(pieces):
+    count = lax.axis_size("tok")
+    return [
+        piece
+        if dist == 0
+        else lax.ppermute(piece, "tok", [(src, src ^ dist) for src in range(count)])
+        for dist, piece in enumerate(pieces)
+    ]
+
+
+def swap_hid(values, dist):
+    count = lax.axis_size("hid")
+    return lax.ppermute(values, "hid", [(src, src ^ dist) for src in range(count)])
+
+
+def in_group_shifts(count):
+    return [0] + [1 << bit for bit in range(count.bit_length() - 1)]
+
+
+def hid_shifts(count):
+    return [1 << bit for bit in range(count.bit_length() - 1)]
+
+
+def column_block(values, index, blk_width):
+    return lax.dynamic_slice_in_dim(
+        values, index * blk_width, blk_width, values.ndim - 1
+    )
+
+
+def fetch_slots(values, code, blk_width):
+    n_tok = lax.axis_size("tok")
+    n_hid = lax.axis_size("hid")
+    me_tok = lax.axis_index("tok")
+    me_hid = lax.axis_index("hid")
+    whole = lax.all_gather(values, "hid", axis=0, tiled=False)
+    group = lax.dynamic_index_in_dim(whole, me_hid ^ (code // n_tok), 0, keepdims=False)
+    shifts = in_group_shifts(n_tok)
+    pieces = [
+        jnp.stack(
+            [
+                column_block(group, me_tok ^ dist ^ (code % n_tok) ^ shift, blk_width)
+                for shift in shifts
+            ]
+        )
+        for dist in range(n_tok)
+    ]
+    got = jnp.concatenate(swap_tok(pieces), axis=1)
+    slots = [got[pos] for pos in range(len(shifts))]
+    slots += [swap_hid(slots[0], dist) for dist in hid_shifts(n_hid)]
+    return jnp.concatenate(slots, axis=1)
+
+
+def return_slots(parts, code, rows, blk_width):
+    n_tok = lax.axis_size("tok")
+    n_hid = lax.axis_size("hid")
+    me_tok = lax.axis_index("tok")
+    me_hid = lax.axis_index("hid")
+    shifts = in_group_shifts(n_tok)
+    base = parts[:, :blk_width]
+    for pos, dist in enumerate(hid_shifts(n_hid)):
+        at = (len(shifts) + pos) * blk_width
+        moved = swap_hid(parts[:, at : at + blk_width].astype(jnp.bfloat16), dist)
+        base = base + moved.astype(jnp.float32)
+    kept = jnp.stack(
+        [base.astype(jnp.bfloat16)]
+        + [
+            parts[:, pos * blk_width : (pos + 1) * blk_width].astype(jnp.bfloat16)
+            for pos in range(1, len(shifts))
+        ]
+    )
+    got = swap_tok([kept[:, dist * rows : (dist + 1) * rows] for dist in range(n_tok)])
+    sums = []
+    for place in range(n_tok):
+        total = 0.0
+        for pos, shift in enumerate(shifts):
+            total = total + got[place ^ shift][pos].astype(jnp.float32)
+        sums.append(total.astype(jnp.bfloat16))
+    whole = lax.all_gather(jnp.stack(sums), "hid", axis=0, tiled=False)
+    group = lax.dynamic_index_in_dim(whole, me_hid ^ (code // n_tok), 0, keepdims=False)
+    return jnp.concatenate(
+        [
+            lax.dynamic_index_in_dim(
+                group, me_tok ^ (code % n_tok) ^ place, 0, keepdims=False
+            )
+            for place in range(n_tok)
+        ],
+        axis=1,
+    )
+
+
+def gather_weights(blocks):
+    n_tok = lax.axis_size("tok")
+    me_tok = lax.axis_index("tok")
+    per = blocks.shape[0] // n_tok
+    deep = blocks.shape[2]
+    got = swap_tok(
+        [
+            lax.dynamic_slice_in_dim(blocks, (me_tok ^ dist) * per, per, 0)
+            for dist in range(n_tok)
+        ]
+    )
+    whole = jnp.zeros((per, blocks.shape[1], deep * n_tok, blocks.shape[3]), blocks.dtype)
+    for dist in range(n_tok):
+        whole = lax.dynamic_update_slice_in_dim(whole, got[dist], (me_tok ^ dist) * deep, 2)
+    return whole
+
+
+def scatter_weights(whole):
+    n_tok = lax.axis_size("tok")
+    me_tok = lax.axis_index("tok")
+    per = whole.shape[0]
+    deep = whole.shape[2] // n_tok
+    got = swap_tok(
+        [
+            lax.dynamic_slice_in_dim(whole, (me_tok ^ dist) * deep, deep, 2)
+            for dist in range(n_tok)
+        ]
+    )
+    blocks = jnp.zeros((per * n_tok, whole.shape[1], deep, whole.shape[3]), whole.dtype)
+    for dist in range(n_tok):
+        blocks = lax.dynamic_update_slice_in_dim(blocks, got[dist], (me_tok ^ dist) * per, 0)
+    return blocks
+
+
+def own_columns(values, blk_width):
+    n_tok = lax.axis_size("tok")
+    me_tok = lax.axis_index("tok")
+    return jnp.concatenate(
+        swap_tok([column_block(values, me_tok ^ dist, blk_width) for dist in range(n_tok)]),
+        axis=0,
+    )
+
+
+def local_moved(
+    tokens,
+    in_blocks,
+    in_left,
+    in_right,
+    in_lists,
+    out_blocks,
+    out_left,
+    out_right,
+    out_lists,
+    cotangent,
+):
+    rows = tokens.shape[0]
+    slots = in_blocks.shape[1]
+    blk = in_blocks.shape[3]
+    n_tok = lax.axis_size("tok")
+    per = in_blocks.shape[0] // n_tok
+    rank = in_left.shape[1]
+    code_in = in_lists[0, 0]
+    code_out = out_lists[0, 0]
+    left_one = lax.all_gather(in_left, "tok", axis=0, tiled=True)
+    right_two = lax.all_gather(out_right, "tok", axis=1, tiled=True)
+    own_in, own_back = rank_sum(
+        (
+            jnp.dot(tokens, left_one, preferred_element_type=jnp.float32),
+            dot_cols(cotangent, right_two),
+        )
+    )
+    own_low = jnp.concatenate(
+        [own_in.astype(jnp.bfloat16), own_back.astype(jnp.bfloat16)], axis=1
+    )
+    low_all = jnp.concatenate(swap_tok([own_low] * n_tok), axis=0)
+    low_in = low_all[:, :rank]
+    low_back = low_all[:, rank:]
+    x_in = fetch_slots(tokens, code_in, blk)
+    x_cot = fetch_slots(cotangent, code_out, blk)
+    tok_own = own_columns(tokens, blk)
+    cot_own = own_columns(cotangent, blk)
+    first = gather_weights(in_blocks).reshape(per, slots * blk, blk)
+    second = gather_weights(out_blocks)
+
+    preact = jnp.concatenate(
+        [jnp.dot(x_in, first[at], preferred_element_type=jnp.float32) for at in range(per)],
+        axis=1,
+    ) + jnp.dot(low_in, in_right, preferred_element_type=jnp.float32)
+    active, slopes = gelu_parts(preact)
+    hidden = active.astype(jnp.bfloat16)
+    hidden_q = [hidden[:, at * blk : (at + 1) * blk] for at in range(per)]
+    grad_hidden = jnp.concatenate(
+        [
+            sum(
+                dot_cols(x_cot[:, k * blk : (k + 1) * blk], second[at, k])
+                for k in range(slots)
+            )
+            for at in range(per)
+        ],
+        axis=1,
+    ) + dot_cols(low_back, out_left)
+    grad_pre = (grad_hidden * slopes).astype(jnp.bfloat16)
+    grad_q = [grad_pre[:, at * blk : (at + 1) * blk] for at in range(per)]
+
+    low_parts = jnp.concatenate(
+        [
+            jnp.dot(hidden, out_left, preferred_element_type=jnp.float32),
+            dot_cols(grad_pre, in_right),
+        ],
+        axis=1,
+    ).astype(jnp.bfloat16)
+    low_got = swap_tok([low_parts[d * rows : (d + 1) * rows] for d in range(n_tok)])
+    low_sum = rank_sum(sum(piece.astype(jnp.float32) for piece in low_got)).astype(
+        jnp.bfloat16
+    )
+    low_mid = low_sum[:, :rank]
+    low_grad = low_sum[:, rank:]
+    low_sum_all = jnp.concatenate(swap_tok([low_sum] * n_tok), axis=0)
+
+    out_parts = jnp.concatenate(
+        [
+            sum(
+                jnp.dot(hidden_q[at], second[at, k], preferred_element_type=jnp.float32)
+                for at in range(per)
+            )
+            for k in range(slots)
+        ],
+        axis=1,
+    )
+    back_parts = sum(dot_cols(grad_q[at], first[at]) for at in range(per))
+    sparse_out = return_slots(out_parts, code_out, rows, blk)
+    sparse_back = return_slots(back_parts, code_in, rows, blk)
+    layer_out = (
+        sparse_out.astype(jnp.float32)
+        + jnp.dot(low_mid, right_two, preferred_element_type=jnp.float32)
+    ).astype(jnp.bfloat16)
+    grad_tokens = (sparse_back.astype(jnp.float32) + dot_cols(low_grad, left_one)).astype(
+        jnp.bfloat16
+    )
+
+    scale = lax.rsqrt(jnp.float32(rows * n_tok))
+    grad_first = jnp.stack(
+        [(scale * dot_rows(x_in, grad_q[at])).astype(jnp.bfloat16) for at in range(per)]
+    ).reshape(per, slots, blk, blk)
+    grad_second = jnp.stack(
+        [
+            jnp.stack(
+                [
+                    (scale * dot_rows(hidden_q[at], x_cot[:, k * blk : (k + 1) * blk])).astype(
+                        jnp.bfloat16
+                    )
+                    for k in range(slots)
+                ]
+            )
+            for at in range(per)
+        ]
+    )
+    return (
+        layer_out,
+        grad_tokens,
+        scatter_weights(grad_first),
+        (scale * dot_rows(tok_own, low_sum_all[:, rank:])).astype(jnp.bfloat16),
+        (scale * dot_rows(low_in, grad_pre)).astype(jnp.bfloat16),
+        scatter_weights(grad_second),
+        (scale * dot_rows(hidden, low_back)).astype(jnp.bfloat16),
+        (scale * dot_rows(low_sum_all[:, :rank], cot_own)).astype(jnp.bfloat16),
+    )
+
+
+def power_of_two(count):
+    return count & (count - 1) == 0
+
+
+def local(*arrays):
+    tokens, in_blocks = arrays[0], arrays[1]
+    n_tok = lax.axis_size("tok")
+    n_hid = lax.axis_size("hid")
+    whole_groups = (
+        power_of_two(n_tok)
+        and power_of_two(n_hid)
+        and tokens.shape[1] == n_tok * in_blocks.shape[3]
+        and in_blocks.shape[0] % n_tok == 0
+    )
+    return local_moved(*arrays) if whole_groups else local_gathered(*arrays)
 
 
 def solution(mesh):

time: 1410 us -> 758 us (0.54)
  waiting for transfers between devices: 1020 us -> 372 us
  local copies, waits for them, and re-layouts: 110 us -> 52.3 us
  starting transfers between devices: 0.56 us -> 56.5 us
  matrix products: 161 us -> 117 us
  blocking collectives: 91.4 us -> 114 us
  other arithmetic: 0.17 us -> 15.3 us
    reduce_scatter x8 -> x0, waiting for transfers between devices: 541 us -> none  [the longest x1 212 us: local(): lax.psum_scatter(terms[1].astype(jnp.bfloat16), 'tok', scatter_dimension=...]
    all_gather x6 -> x4, waiting for transfers between devices: 471 us -> 0.01 us  [the longest x2 0.01 us: fetch_slots(): whole = lax.all_gather(values, 'hid', axis=0, tiled=False)]
    ppermute x0 -> x51, waiting for transfers between devices: none -> 370 us  [the longest x39 369 us: swap_tok(): lax.ppermute(piece, 'tok', [(src, src ^ dist) for src in range(count)])]
    dot_general x12 -> x32, matrix products: 143 us -> 38.3 us  [the longest x24 30.2 us: local_moved(): jnp.dot(hidden_q[at], second[at, k], preferred_element_type=jnp.float32)]
    ppermute x0 -> x51, starting transfers between devices: none -> 56.2 us  [the longest x39 45.9 us: swap_tok(): lax.ppermute(piece, 'tok', [(src, src ^ dist) for src in range(count)])]
    dot_general x4 -> x32, matrix products: 9.55 us -> 53 us  [dot_cols(): lax.dot_general(left_arr, right_arr, (((1,), (1,)), ((), ())), preferred_...]
    unnamed x42 -> x105, local copies, waits for them, and re-layouts: 45.4 us -> 5.97 us
    convert_element_type x2 -> x0, local copies, waits for them, and re-layouts: 34.6 us -> none  [the longest x1 17.8 us: local(): terms[1].astype(jnp.bfloat16)]
  transfers between devices with their start and end apart: 14 -> 55, of which waited for: 11 -> 27; matrix products, arithmetic and copies ran while one was open for 19% -> 24% of each run, Pallas kernels for 0% -> 0%
where the time goes in v1:
time: 758 us; the launch traced here: 747 us
  waiting for transfers between devices  372 us (49%)
  matrix products  117 us (15%)
  blocking collectives  114 us (15%)
  starting transfers between devices  56.5 us (7%)
  local copies, waits for them, and re-layouts  52.3 us (7%)
  between operations  20.4 us (3%)
  other arithmetic  15.3 us (2%)
    ppermute x39, waiting for transfers between devices, swap_tok(): lax.ppermute(piece, 'tok', [(src, src ^ dist) for src in range(count)])  369 us
    psum x2, blocking collectives, rank_sum(): return lax.psum(values, 'hid')  73.1 us
    dot_general x32, matrix products, dot_cols(): lax.dot_general(left_arr, right_arr, (((1,), (1,)), ((), ())), preferred_...  53 us
    ppermute x39, starting transfers between devices, swap_tok(): lax.ppermute(piece, 'tok', [(src, src ^ dist) for src in range(count)])  45.9 us
    dot_general x24, matrix products, local_moved(): jnp.dot(hidden_q[at], second[at, k], preferred_element_type=jnp.float32)  30.2 us
    all_gather x1, blocking collectives, local_moved(): right_two = lax.all_gather(out_right, 'tok', axis=1, tiled=True)  27.9 us
    dot_general x32, matrix products, dot_rows(): lax.dot_general(left_arr, right_arr, (((0,), (0,)), ((), ())), preferred_...  25.2 us
  transfers between devices with their start and end apart: 55, of which 27 were waited for; matrix products, arithmetic and copies ran while one was open for 24% of the time, Pallas kernels for 0%

profile of v1, /device:TPU:11, one launch (start us, length us, event | category | flops | bytes accessed | tf_op | source)
XLA Modules:
  0.0 746.5 jit_solution(9998169249330070195)
XLA Ops:
  8.8 2.0 broadcast.25.clone
  13.4 27.9 %all_gather.33 = bf16[256,1024]{1,0:T(8,128)(2,1)S(1)} all-gather(bf16[256,256]{1,0:T(8,128)(2,1)S(1)} %copy-done.38), channel_id=1, replica_groups=mesh['hid'=8,'tok'=4] {'tok'}, dimensions={1}, use_global_device_ids=true | all-gather | bytes 655360 | tf_op jit(solution)/shard_map/all_gather | solution.py:337
  42.4 12.7 %all_gather.32 = bf16[1024,256]{1,0:T(8,128)(2,1)S(1)} all-gather(bf16[256,256]{1,0:T(8,128)(2,1)S(1)} %copy-done.39), channel_id=1, replica_groups=mesh['hid'=8,'tok'=4] {'tok'}, dimensions={0}, use_global_device_ids=true | all-gather | bytes 655360 | tf_op jit(solution)/shard_map/all_gather | solution.py:336
  56.2 38.9 %all-reduce.3 = (bf16[224,256]{1,0:T(8,128)(2,1)}, bf16[224,256]{1,0:T(8,128)(2,1)}) all-reduce(f32[224,256]{1,0:T(8,128)S(1)} %fusion.276, f32[224,256]{1,0:T(8,128)S(1)} %fusion.275), channel_id=1, replica_groups=mesh['hid'=8,'tok'=4] {'hid'}, use_global_device_ids=true, to_apply=%region_1.0 | all-reduce | flops 114688 | bytes 688128 | tf_op jit(solution)/shard_map/psum | solution.py:35
  95.1 1.8 pad_maximum_fusion.23
  96.9 2.0 broadcast.25.clone.1
  98.9 1.9 constant_dynamic-slice_fusion.28
  100.9 3.5 collective-permute-start.6
  104.4 2.4 collective-permute-start.13
  106.8 3.0 collective-permute-done.11
  117.5 10.1 %collective-permute-done.10 = bf16[224,512]{1,0:T(8,128)(2,1)} collective-permute-done((bf16[224,512]{1,0:T(8,128)(2,1)}, bf16[224,512]{1,0:T(8,128)(2,1)}, u32[]{:S(2)}, u32[]{:S(2)}) %collective-permute-start.10) | collective-permute-done | bytes 229408 | tf_op jit(solution)/shard_map/ppermute | solution.py:188
  128.4 22.1 %collective-permute-done.9 = bf16[224,512]{1,0:T(8,128)(2,1)} collective-permute-done((bf16[224,512]{1,0:T(8,128)(2,1)}, bf16[224,512]{1,0:T(8,128)(2,1)}, u32[]{:S(2)}, u32[]{:S(2)}) %collective-permute-start.9) | collective-permute-done | bytes 229408 | tf_op jit(solution)/shard_map/ppermute | solution.py:188
  152.8 2.1 pad_maximum_fusion.4
  154.9 2.1 constant_dynamic-update-slice_fusion.12
  157.0 2.1 constant_dynamic-update-slice_fusion.15
  159.1 44.9 %collective-permute-done.13 = bf16[4,6,64,256]{3,2,1,0:T(8,128)(2,1)} collective-permute-done((bf16[4,6,64,256]{3,2,1,0:T(8,128)(2,1)S(1)}, bf16[4,6,64,256]{3,2,1,0:T(8,128)(2,1)}, u32[]{:S(2)}, u32[]{:S(2)}) %collective-permute-start.13) | collective-permute-done | bytes 786464 | tf_op jit(solution)/shard_map/ppermute | solution.py:188
  204.0 3.2 collective-permute-start.40
  207.2 2.1 constant_dynamic-update-slice_fusion.11
  209.3 14.1 %collective-permute-done.7 = bf16[4,6,64,256]{3,2,1,0:T(8,128)(2,1)} collective-permute-done((bf16[4,6,64,256]{3,2,1,0:T(8,128)(2,1)}, bf16[4,6,64,256]{3,2,1,0:T(8,128)(2,1)}, u32[]{:S(2)}, u32[]{:S(2)}) %collective-permute-start.7) | collective-permute-done | bytes 786464 | tf_op jit(solution)/shard_map/ppermute | solution.py:188
  223.4 2.1 constant_dynamic-update-slice_fusion.14
  225.5 24.3 %collective-permute-done.14 = bf16[4,6,64,256]{3,2,1,0:T(8,128)(2,1)S(1)} collective-permute-done((bf16[4,6,64,256]{3,2,1,0:T(8,128)(2,1)S(1)}, bf16[4,6,64,256]{3,2,1,0:T(8,128)(2,1)S(1)}, u32[]{:S(2)}, u32[]{:S(2)}) %collective-permute-start.14) | collective-permute-done | bytes 786464 | tf_op jit(solution)/shard_map/ppermute | solution.py:188
  250.7 16.0 %collective-permute-done.8 = bf16[4,6,64,256]{3,2,1,0:T(8,128)(2,1)S(1)} collective-permute-done((bf16[4,6,64,256]{3,2,1,0:T(8,128)(2,1)}, bf16[4,6,64,256]{3,2,1,0:T(8,128)(2,1)S(1)}, u32[]{:S(2)}, u32[]{:S(2)}) %collective-permute-start.8) | collective-permute-done | bytes 786464 | tf_op jit(solution)/shard_map/ppermute | solution.py:188
  267.7 3.3 fusion.268
  271.0 2.8 constant_dynamic-slice_fusion.43
  274.8 2.6 collective-permute-start
  277.4 2.4 constant_dynamic-slice_fusion.23
  280.0 11.3 %collective-permute-done.2 = bf16[3,224,256]{2,1,0:T(8,128)(2,1)} collective-permute-done((bf16[3,224,256]{2,1,0:T(8,128)(2,1)S(1)}, bf16[3,224,256]{2,1,0:T(8,128)(2,1)}, u32[]{:S(2)}, u32[]{:S(2)}) %collective-permute-start.2) | collective-permute-done | bytes 344096 | tf_op jit(solution)/shard_map/ppermute | solution.py:188
  291.5 12.4 %collective-permute-done.1 = bf16[3,224,256]{2,1,0:T(8,128)(2,1)} collective-permute-done((bf16[3,224,256]{2,1,0:T(8,128)(2,1)S(1)}, bf16[3,224,256]{2,1,0:T(8,128)(2,1)}, u32[]{:S(2)}, u32[]{:S(2)}) %collective-permute-start.1) | collective-permute-done | bytes 344096 | tf_op jit(solution)/shard_map/ppermute | solution.py:188
  303.9 3.1 collective-permute-start.22
  308.5 12.1 %collective-permute-done.23 = bf16[3,224,256]{2,1,0:T(8,128)(2,1)S(1)} collective-permute-done((bf16[3,224,256]{2,1,0:T(8,128)(2,1)S(1)}, bf16[3,224,256]{2,1,0:T(8,128)(2,1)S(1)}, u32[]{:S(2)}, u32[]{:S(2)}) %collective-permute-start.23) | collective-permute-done | bytes 344096 | tf_op jit(solution)/shard_map/ppermute | solution.py:188
  321.5 4.6 collective-permute-done.22
  345.3 1.9 multiply_convert_fusion
  395.1 3.6 fusion.6
  398.7 3.3 fusion.157
  404.5 3.3 fusion.163
  409.4 3.2 collective-permute-start.19
  414.1 3.3 fusion.160
  417.4 10.4 %collective-permute-done.19 = bf16[3,224,256]{2,1,0:T(8,128)(2,1)S(1)} collective-permute-done((bf16[3,224,256]{2,1,0:T(8,128)(2,1)S(1)}, bf16[3,224,256]{2,1,0:T(8,128)(2,1)S(1)}, u32[]{:S(2)}, u32[]{:S(2)}) %collective-permute-start.19) | collective-permute-done | bytes 344096 | tf_op jit(solution)/shard_map/ppermute | solution.py:188
  428.6 14.7 %collective-permute-done.20 = bf16[3,224,256]{2,1,0:T(8,128)(2,1)S(1)} collective-permute-done((bf16[3,224,256]{2,1,0:T(8,128)(2,1)S(1)}, bf16[3,224,256]{2,1,0:T(8,128)(2,1)S(1)}, u32[]{:S(2)}, u32[]{:S(2)}) %collective-permute-start.20) | collective-permute-done | bytes 344096 | tf_op jit(solution)/shard_map/ppermute | solution.py:188
  444.6 7.2 fusion.270
  452.8 1.7 collective-permute-start.31
  469.1 2.8 collective-permute-start.33
  473.2 2.1 pad_maximum_fusion
  475.3 7.8 %collective-permute-done.34 = bf16[3,224,256]{2,1,0:T(8,128)(2,1)S(1)} collective-permute-done((bf16[3,224,256]{2,1,0:T(8,128)(2,1)S(1)}, bf16[3,224,256]{2,1,0:T(8,128)(2,1)S(1)}, u32[]{:S(2)}, u32[]{:S(2)}) %collective-permute-start.34) | collective-permute-done | bytes 344096 | tf_op jit(solution)/shard_map/ppermute | solution.py:188
  483.1 2.2 collective-permute-start.29
  486.6 2.7 collective-permute-start.28
  489.4 22.6 %collective-permute-done.35 = bf16[3,224,256]{2,1,0:T(8,128)(2,1)S(1)} collective-permute-done((bf16[3,224,256]{2,1,0:T(8,128)(2,1)S(1)}, bf16[3,224,256]{2,1,0:T(8,128)(2,1)S(1)}, u32[]{:S(2)}, u32[]{:S(2)}) %collective-permute-start.35) | collective-permute-done | bytes 344096 | tf_op jit(solution)/shard_map/ppermute | solution.py:188
  513.1 2.1 broadcast.29.clone
  516.2 1.7 constant_dynamic-slice_fusion.8
  535.4 34.2 %all-reduce.4 = bf16[224,512]{0,1:T(8,128)(2,1)S(1)} all-reduce(f32[224,512]{0,1:T(8,128)S(1)} %convert_add_fusion), channel_id=1, replica_groups=mesh['hid'=8,'tok'=4] {'hid'}, use_global_device_ids=true, to_apply=%region_2.3 | all-reduce | flops 114688 | bytes 688128 | tf_op jit(solution)/shard_map/psum | solution.py:35
  574.7 2.4 collective-permute-start.37
  577.1 2.1 broadcast.29.clone.1
  580.4 8.8 %collective-permute-done.44 = bf16[224,512]{0,1:T(8,128)(2,1)S(1)} collective-permute-done((bf16[224,512]{0,1:T(8,128)(2,1)S(1)}, bf16[224,512]{0,1:T(8,128)(2,1)S(1)}, u32[]{:S(2)}, u32[]{:S(2)}) %collective-permute-start.44) | collective-permute-done | bytes 229408 | tf_op jit(solution)/shard_map/ppermute | solution.py:188
  589.2 23.9 %collective-permute-done.43 = bf16[224,512]{0,1:T(8,128)(2,1)S(1)} collective-permute-done((bf16[224,512]{0,1:T(8,128)(2,1)S(1)}, bf16[224,512]{0,1:T(8,128)(2,1)S(1)}, u32[]{:S(2)}, u32[]{:S(2)}) %collective-permute-start.43) | collective-permute-done | bytes 229408 | tf_op jit(solution)/shard_map/ppermute | solution.py:188
  613.1 2.3 collective-permute-start.48
  616.9 32.4 %collective-permute-done.49 = bf16[224,256]{1,0:T(8,128)(2,1)S(1)} collective-permute-done((bf16[224,256]{1,0:T(8,128)(2,1)S(1)}, bf16[224,256]{1,0:T(8,128)(2,1)S(1)}, u32[]{:S(2)}, u32[]{:S(2)}) %collective-permute-start.49) | collective-permute-done | bytes 114720 | tf_op jit(solution)/shard_map/ppermute | solution.py:188
  649.3 2.0 collective-permute-start.45
  651.5 3.2 collective-permute-start.46
  654.8 1.9 fusion.55
  657.8 2.1 constant_dynamic-update-slice_fusion.9
  660.8 6.3 collective-permute-done.38
  668.1 3.1 collective-permute-done.45
  672.1 44.6 %collective-permute-done.46 = bf16[4,6,64,256]{3,2,1,0:T(8,128)(2,1)S(1)} collective-permute-done((bf16[4,6,64,256]{3,2,1,0:T(8,128)(2,1)S(1)}, bf16[4,6,64,256]{3,2,1,0:T(8,128)(2,1)S(1)}, u32[]{:S(2)}, u32[]{:S(2)}) %collective-permute-start.46) | collective-permute-done | bytes 786464 | tf_op jit(solution)/shard_map/ppermute | solution.py:188
  717.7 16.7 %collective-permute-done.47 = bf16[4,6,64,256]{3,2,1,0:T(8,128)(2,1)S(1)} collective-permute-done((bf16[4,6,64,256]{3,2,1,0:T(8,128)(2,1)S(1)}, bf16[4,6,64,256]{3,2,1,0:T(8,128)(2,1)S(1)}, u32[]{:S(2)}, u32[]{:S(2)}) %collective-permute-start.47) | collective-permute-done | bytes 786464 | tf_op jit(solution)/shard_map/ppermute | solution.py:188
  (310 shorter events, 147.8 us)
Async XLA Ops:
  7.2 338.1 %copy-start = (bf16[256,1024]{1,0:T(8,128)(2,1)S(1)}, bf16[256,1024]{1,0:T(8,128)(2,1)}, u32[]{:S(2)}) copy-start(bf16[256,1024]{1,0:T(8,128)(2,1)} %param.13) | copy-start | bytes 1572868
  7.2 263.8 %all-gather.9.cloned.1.call-start = ((), (), s32[]{:S(2)}) async-start(), calls=%async_computation | async-start | bytes 4128768 | tf_op jit(solution)/shard_map/all_gather | solution.py:217
  7.9 269.5 %all-gather.13.cloned.1.call-start = ((), (), s32[]{:S(2)}) async-start(), calls=%async_computation.2 | async-start | bytes 4128768 | tf_op jit(solution)/shard_map/all_gather | solution.py:217
  8.7 726.7 %all-gather.11.cloned.1.call-start = ((), (), s32[]{:S(2)}) async-start(), calls=%async_computation.1 | async-start | bytes 4128768 | tf_op jit(solution)/shard_map/all_gather | solution.py:260
  13.2 138.1 %collective-permute-start.12 = (bf16[4,6,64,256]{3,2,1,0:T(8,128)(2,1)}, bf16[4,6,64,256]{3,2,1,0:T(8,128)(2,1)}, u32[]{:S(2)}, u32[]{:S(2)}) collective-permute-start(bf16[4,6,64,256]{3,2,1,0:T(8,128)(2,1)} %get-tuple-element.59), channel_id=1, source_target_pairs={{0,1},{1,0},{2,3},{3,2},{4,5},{5,4},{6,7},{7,6},{8,9},{9,8},{10,11... | collective-permute-start | bytes 2359304 | tf_op jit(solution)/shard_map/ppermute | solution.py:188
  96.9 12.9 %collective-permute-start.11 = (bf16[224,512]{1,0:T(8,128)(2,1)}, bf16[224,512]{1,0:T(8,128)(2,1)S(1)}, u32[]{:S(2)}, u32[]{:S(2)}) collective-permute-start(bf16[224,512]{1,0:T(8,128)(2,1)} %pad_maximum_fusion.23), channel_id=1, source_target_pairs={{0,3},{1,2},{2,1},{3,0},{4,7},{5,6},{6,5},{7,4},{8,11},{9,10},{10,... | collective-permute-start | bytes 688136 | tf_op jit(solution)/shard_map/ppermute | solution.py:188
  98.9 53.8 %copy-start.36 = (bf16[224,256]{1,0:T(8,128)(2,1)S(1)}, bf16[224,256]{1,0:T(8,128)(2,1)}, u32[]{:S(2)}) copy-start(bf16[224,256]{1,0:T(8,128)(2,1)} %get-tuple-element.8) | copy-start | bytes 344068
  98.9 53.8 %copy-start.37 = (bf16[224,256]{1,0:T(8,128)(2,1)S(1)}, bf16[224,256]{1,0:T(8,128)(2,1)}, u32[]{:S(2)}) copy-start(bf16[224,256]{1,0:T(8,128)(2,1)} %get-tuple-element.9) | copy-start | bytes 344068
  100.9 56.1 %collective-permute-start.6 = (bf16[4,6,64,256]{3,2,1,0:T(8,128)(2,1)}, bf16[4,6,64,256]{3,2,1,0:T(8,128)(2,1)}, u32[]{:S(2)}, u32[]{:S(2)}) collective-permute-start(bf16[4,6,64,256]{3,2,1,0:T(8,128)(2,1)} %get-tuple-element.55), channel_id=1, source_target_pairs={{0,1},{1,0},{2,3},{3,2},{4,5},{5,4},{6,7},{7,6},{8,9},{9,8},{10,11... | collective-permute-start | bytes 2359304 | tf_op jit(solution)/shard_map/ppermute | solution.py:188
  104.4 23.2 %collective-permute-start.10 = (bf16[224,512]{1,0:T(8,128)(2,1)}, bf16[224,512]{1,0:T(8,128)(2,1)}, u32[]{:S(2)}, u32[]{:S(2)}) collective-permute-start(bf16[224,512]{1,0:T(8,128)(2,1)} %pad_maximum_fusion.23), channel_id=1, source_target_pairs={{0,2},{1,3},{2,0},{3,1},{4,6},{5,7},{6,4},{7,5},{8,10},{9,11},{10,... | collective-permute-start | bytes 688136 | tf_op jit(solution)/shard_map/ppermute | solution.py:188
  104.4 99.6 %collective-permute-start.13 = (bf16[4,6,64,256]{3,2,1,0:T(8,128)(2,1)S(1)}, bf16[4,6,64,256]{3,2,1,0:T(8,128)(2,1)}, u32[]{:S(2)}, u32[]{:S(2)}) collective-permute-start(bf16[4,6,64,256]{3,2,1,0:T(8,128)(2,1)S(1)} %get-tuple-element.61), channel_id=1, source_target_pairs={{0,2},{1,3},{2,0},{3,1},{4,6},{5,7},{6,4},{7,5},{8,10},{9,11},{10,... | collective-permute-start | bytes 2359304 | tf_op jit(solution)/shard_map/ppermute | solution.py:188
  109.8 40.7 %collective-permute-start.9 = (bf16[224,512]{1,0:T(8,128)(2,1)}, bf16[224,512]{1,0:T(8,128)(2,1)}, u32[]{:S(2)}, u32[]{:S(2)}) collective-permute-start(bf16[224,512]{1,0:T(8,128)(2,1)} %pad_maximum_fusion.23), channel_id=1, source_target_pairs={{0,1},{1,0},{2,3},{3,2},{4,5},{5,4},{6,7},{7,6},{8,9},{9,8},{10,11... | collective-permute-start | bytes 688136 | tf_op jit(solution)/shard_map/ppermute | solution.py:188
  127.6 95.8 %collective-permute-start.7 = (bf16[4,6,64,256]{3,2,1,0:T(8,128)(2,1)}, bf16[4,6,64,256]{3,2,1,0:T(8,128)(2,1)}, u32[]{:S(2)}, u32[]{:S(2)}) collective-permute-start(bf16[4,6,64,256]{3,2,1,0:T(8,128)(2,1)} %get-tuple-element.57), channel_id=1, source_target_pairs={{0,2},{1,3},{2,0},{3,1},{4,6},{5,7},{6,4},{7,5},{8,10},{9,11},{10,... | collective-permute-start | bytes 2359304 | tf_op jit(solution)/shard_map/ppermute | solution.py:188
  150.5 99.3 %collective-permute-start.14 = (bf16[4,6,64,256]{3,2,1,0:T(8,128)(2,1)S(1)}, bf16[4,6,64,256]{3,2,1,0:T(8,128)(2,1)S(1)}, u32[]{:S(2)}, u32[]{:S(2)}) collective-permute-start(bf16[4,6,64,256]{3,2,1,0:T(8,128)(2,1)S(1)} %get-tuple-element.58), channel_id=1, source_target_pairs={{0,3},{1,2},{2,1},{3,0},{4,7},{5,6},{6,5},{7,4},{8,11},{9,10},{10,... | collective-permute-start | bytes 2359304 | tf_op jit(solution)/shard_map/ppermute | solution.py:188
  151.3 115.5 %collective-permute-start.8 = (bf16[4,6,64,256]{3,2,1,0:T(8,128)(2,1)}, bf16[4,6,64,256]{3,2,1,0:T(8,128)(2,1)S(1)}, u32[]{:S(2)}, u32[]{:S(2)}) collective-permute-start(bf16[4,6,64,256]{3,2,1,0:T(8,128)(2,1)} %get-tuple-element.54), channel_id=1, source_target_pairs={{0,3},{1,2},{2,1},{3,0},{4,7},{5,6},{6,5},{7,4},{8,11},{9,10},{10,... | collective-permute-start | bytes 2359304 | tf_op jit(solution)/shard_map/ppermute | solution.py:188
  157.0 412.6 %collective-permute-start.41 = (bf16[224,256]{1,0:T(8,128)(2,1)}, bf16[224,256]{1,0:T(8,128)(2,1)}, u32[]{:S(2)}, u32[]{:S(2)}) collective-permute-start(bf16[224,256]{1,0:T(8,128)(2,1)} %get-tuple-element.90), channel_id=1, source_target_pairs={{0,3},{1,2},{2,1},{3,0},{4,7},{5,6},{6,5},{7,4},{8,11},{9,10},{10,... | collective-permute-start | bytes 344072 | tf_op jit(solution)/shard_map/ppermute | solution.py:188
  204.0 366.8 %collective-permute-start.40 = (bf16[224,256]{1,0:T(8,128)(2,1)}, bf16[224,256]{1,0:T(8,128)(2,1)S(1)}, u32[]{:S(2)}, u32[]{:S(2)}) collective-permute-start(bf16[224,256]{1,0:T(8,128)(2,1)} %get-tuple-element.91), channel_id=1, source_target_pairs={{0,2},{1,3},{2,0},{3,1},{4,6},{5,7},{6,4},{7,5},{8,10},{9,11},{10,... | collective-permute-start | bytes 344072 | tf_op jit(solution)/shard_map/ppermute | solution.py:188
  271.0 70.0 %copy-start.11 = (bf16[1,6,256,256]{3,2,1,0:T(8,128)(2,1)}, bf16[1,6,256,256]{3,2,1,0:T(8,128)(2,1)S(1)}, u32[]{:S(2)}) copy-start(bf16[1,6,256,256]{3,2,1,0:T(8,128)(2,1)S(1)} %get-tuple-element.51) | copy-start | bytes 2359300
  271.0 72.1 %copy-start.14 = (bf16[1,6,256,256]{3,2,1,0:T(8,128)(2,1)}, bf16[1,6,256,256]{3,2,1,0:T(8,128)(2,1)S(1)}, u32[]{:S(2)}) copy-start(bf16[1,6,256,256]{3,2,1,0:T(8,128)(2,1)S(1)} %get-tuple-element.53) | copy-start | bytes 2359300
  273.8 17.4 %collective-permute-start.2 = (bf16[3,224,256]{2,1,0:T(8,128)(2,1)S(1)}, bf16[3,224,256]{2,1,0:T(8,128)(2,1)}, u32[]{:S(2)}, u32[]{:S(2)}) collective-permute-start(bf16[3,224,256]{2,1,0:T(8,128)(2,1)S(1)} %pad_maximum_fusion.18), channel_id=1, source_target_pairs={{0,3},{1,2},{2,1},{3,0},{4,7},{5,6},{6,5},{7,4},{8,11},{9,10},{10,... | collective-permute-start | bytes 1032200 | tf_op jit(solution)/shard_map/ppermute | solution.py:188
  274.0 29.9 %collective-permute-start.1 = (bf16[3,224,256]{2,1,0:T(8,128)(2,1)S(1)}, bf16[3,224,256]{2,1,0:T(8,128)(2,1)}, u32[]{:S(2)}, u32[]{:S(2)}) collective-permute-start(bf16[3,224,256]{2,1,0:T(8,128)(2,1)S(1)} %pad_maximum_fusion.17), channel_id=1, source_target_pairs={{0,2},{1,3},{2,0},{3,1},{4,6},{5,7},{6,4},{7,5},{8,10},{9,11},{10,... | collective-permute-start | bytes 1032200 | tf_op jit(solution)/shard_map/ppermute | solution.py:188
  274.8 32.2 %collective-permute-start = (bf16[3,224,256]{2,1,0:T(8,128)(2,1)}, bf16[3,224,256]{2,1,0:T(8,128)(2,1)}, u32[]{:S(2)}, u32[]{:S(2)}) collective-permute-start(bf16[3,224,256]{2,1,0:T(8,128)(2,1)} %pad_maximum_fusion.16), channel_id=1, source_target_pairs={{0,1},{1,0},{2,3},{3,2},{4,5},{5,4},{6,7},{7,6},{8,9},{9,8},{10,11... | collective-permute-start | bytes 1032200 | tf_op jit(solution)/shard_map/ppermute | solution.py:188
  291.2 29.4 %collective-permute-start.23 = (bf16[3,224,256]{2,1,0:T(8,128)(2,1)S(1)}, bf16[3,224,256]{2,1,0:T(8,128)(2,1)S(1)}, u32[]{:S(2)}, u32[]{:S(2)}) collective-permute-start(bf16[3,224,256]{2,1,0:T(8,128)(2,1)S(1)} %pad_maximum_fusion.21), channel_id=1, source_target_pairs={{0,3},{1,2},{2,1},{3,0},{4,7},{5,6},{6,5},{7,4},{8,11},{9,10},{10,... | collective-permute-start | bytes 1032200 | tf_op jit(solution)/shard_map/ppermute | solution.py:188
  303.9 22.1 %collective-permute-start.22 = (bf16[3,224,256]{2,1,0:T(8,128)(2,1)S(1)}, bf16[3,224,256]{2,1,0:T(8,128)(2,1)S(1)}, u32[]{:S(2)}, u32[]{:S(2)}) collective-permute-start(bf16[3,224,256]{2,1,0:T(8,128)(2,1)S(1)} %pad_maximum_fusion.20), channel_id=1, source_target_pairs={{0,2},{1,3},{2,0},{3,1},{4,6},{5,7},{6,4},{7,5},{8,10},{9,11},{10,... | collective-permute-start | bytes 1032200 | tf_op jit(solution)/shard_map/ppermute | solution.py:188
  307.0 19.0 %collective-permute-start.21 = (bf16[3,224,256]{2,1,0:T(8,128)(2,1)S(1)}, bf16[3,224,256]{2,1,0:T(8,128)(2,1)S(1)}, u32[]{:S(2)}, u32[]{:S(2)}) collective-permute-start(bf16[3,224,256]{2,1,0:T(8,128)(2,1)S(1)} %pad_maximum_fusion.19), channel_id=1, source_target_pairs={{0,1},{1,0},{2,3},{3,2},{4,5},{5,4},{6,7},{7,6},{8,9},{9,8},{10,11... | collective-permute-start | bytes 1032200 | tf_op jit(solution)/shard_map/ppermute | solution.py:188
  320.6 16.2 %collective-permute-start.3 = (bf16[896,256]{1,0:T(8,128)(2,1)S(1)}, bf16[896,256]{1,0:T(8,128)(2,1)S(1)}, u32[]{:S(2)}, u32[]{:S(2)}) collective-permute-start(bf16[896,256]{1,0:T(8,128)(2,1)S(1)} %slice_bitcast_fusion.7), channel_id=1, source_target_pairs={{0,4},{4,0},{8,12},{12,8},{16,20},{20,16},{24,28},{28,24},{1,5},{5... | collective-permute-start | bytes 1376264 | tf_op jit(solution)/shard_map/ppermute | solution.py:195
  326.0 11.9 %collective-permute-start.4 = (bf16[896,256]{1,0:T(8,128)(2,1)S(1)}, bf16[896,256]{1,0:T(8,128)(2,1)S(1)}, u32[]{:S(2)}, u32[]{:S(2)}) collective-permute-start(bf16[896,256]{1,0:T(8,128)(2,1)S(1)} %slice_bitcast_fusion.7), channel_id=1, source_target_pairs={{0,8},{4,12},{8,0},{12,4},{16,24},{20,28},{24,16},{28,20},{1,9},{5... | collective-permute-start | bytes 1376264 | tf_op jit(solution)/shard_map/ppermute | solution.py:195
  326.0 13.4 %collective-permute-start.5 = (bf16[896,256]{1,0:T(8,128)(2,1)S(1)}, bf16[896,256]{1,0:T(8,128)(2,1)S(1)}, u32[]{:S(2)}, u32[]{:S(2)}) collective-permute-start(bf16[896,256]{1,0:T(8,128)(2,1)S(1)} %slice_bitcast_fusion.7), channel_id=1, source_target_pairs={{0,16},{4,20},{8,24},{12,28},{16,0},{20,4},{24,8},{28,12},{1,17},{... | collective-permute-start | bytes 1376264 | tf_op jit(solution)/shard_map/ppermute | solution.py:195
  326.7 67.0 %copy-start.1 = (bf16[3,896,256]{2,1,0:T(8,128)(2,1)}, bf16[3,896,256]{2,1,0:T(8,128)(2,1)S(1)}, u32[]{:S(2)}) copy-start(bf16[3,896,256]{2,1,0:T(8,128)(2,1)S(1)} %pad_maximum_fusion.3) | copy-start | bytes 4128772
  336.9 34.1 %collective-permute-start.26 = (bf16[896,256]{1,0:T(8,128)(2,1)S(1)}, bf16[896,256]{1,0:T(8,128)(2,1)S(1)}, u32[]{:S(2)}, u32[]{:S(2)}) collective-permute-start(bf16[896,256]{1,0:T(8,128)(2,1)S(1)} %slice_bitcast_fusion.4), channel_id=1, source_target_pairs={{0,16},{4,20},{8,24},{12,28},{16,0},{20,4},{24,8},{28,12},{1,17},{... | collective-permute-start | bytes 1376264 | tf_op jit(solution)/shard_map/ppermute | solution.py:195
  337.9 36.2 %collective-permute-start.25 = (bf16[896,256]{1,0:T(8,128)(2,1)S(1)}, bf16[896,256]{1,0:T(8,128)(2,1)S(1)}, u32[]{:S(2)}, u32[]{:S(2)}) collective-permute-start(bf16[896,256]{1,0:T(8,128)(2,1)S(1)} %slice_bitcast_fusion.4), channel_id=1, source_target_pairs={{0,8},{4,12},{8,0},{12,4},{16,24},{20,28},{24,16},{28,20},{1,9},{5... | collective-permute-start | bytes 1376264 | tf_op jit(solution)/shard_map/ppermute | solution.py:195
  339.5 37.3 %collective-permute-start.24 = (bf16[896,256]{1,0:T(8,128)(2,1)S(1)}, bf16[896,256]{1,0:T(8,128)(2,1)S(1)}, u32[]{:S(2)}, u32[]{:S(2)}) collective-permute-start(bf16[896,256]{1,0:T(8,128)(2,1)S(1)} %slice_bitcast_fusion.4), channel_id=1, source_target_pairs={{0,4},{4,0},{8,12},{12,8},{16,20},{20,16},{24,28},{28,24},{1,5},{5... | collective-permute-start | bytes 1376264 | tf_op jit(solution)/shard_map/ppermute | solution.py:195
  371.0 36.9 %collective-permute-start.17 = (bf16[896,256]{1,0:T(8,128)(2,1)S(1)}, bf16[896,256]{1,0:T(8,128)(2,1)S(1)}, u32[]{:S(2)}, u32[]{:S(2)}) collective-permute-start(bf16[896,256]{1,0:T(8,128)(2,1)S(1)} %fusion.46), channel_id=1, source_target_pairs={{0,16},{4,20},{8,24},{12,28},{16,0},{20,4},{24,8},{28,12},{1,17},{... | collective-permute-start | bytes 1376264 | tf_op jit(solution)/shard_map/ppermute | solution.py:195
  374.1 33.7 %collective-permute-start.16 = (bf16[896,256]{1,0:T(8,128)(2,1)S(1)}, bf16[896,256]{1,0:T(8,128)(2,1)S(1)}, u32[]{:S(2)}, u32[]{:S(2)}) collective-permute-start(bf16[896,256]{1,0:T(8,128)(2,1)S(1)} %fusion.45), channel_id=1, source_target_pairs={{0,8},{4,12},{8,0},{12,4},{16,24},{20,28},{24,16},{28,20},{1,9},{5... | collective-permute-start | bytes 1376264 | tf_op jit(solution)/shard_map/ppermute | solution.py:195
  376.8 31.0 %collective-permute-start.15 = (bf16[896,256]{1,0:T(8,128)(2,1)S(1)}, bf16[896,256]{1,0:T(8,128)(2,1)S(1)}, u32[]{:S(2)}, u32[]{:S(2)}) collective-permute-start(bf16[896,256]{1,0:T(8,128)(2,1)S(1)} %fusion.44), channel_id=1, source_target_pairs={{0,4},{4,0},{8,12},{12,8},{16,20},{20,16},{24,28},{28,24},{1,5},{5... | collective-permute-start | bytes 1376264 | tf_op jit(solution)/shard_map/ppermute | solution.py:195
  409.4 18.4 %collective-permute-start.19 = (bf16[3,224,256]{2,1,0:T(8,128)(2,1)S(1)}, bf16[3,224,256]{2,1,0:T(8,128)(2,1)S(1)}, u32[]{:S(2)}, u32[]{:S(2)}) collective-permute-start(bf16[3,224,256]{2,1,0:T(8,128)(2,1)S(1)} %get-tuple-element.71), channel_id=1, source_target_pairs={{0,2},{1,3},{2,0},{3,1},{4,6},{5,7},{6,4},{7,5},{8,10},{9,11},{10,... | collective-permute-start | bytes 1032200 | tf_op jit(solution)/shard_map/ppermute | solution.py:188
  412.6 16.0 %collective-permute-start.18 = (bf16[3,224,256]{2,1,0:T(8,128)(2,1)S(1)}, bf16[3,224,256]{2,1,0:T(8,128)(2,1)S(1)}, u32[]{:S(2)}, u32[]{:S(2)}) collective-permute-start(bf16[3,224,256]{2,1,0:T(8,128)(2,1)S(1)} %get-tuple-element.72), channel_id=1, source_target_pairs={{0,1},{1,0},{2,3},{3,2},{4,5},{5,4},{6,7},{7,6},{8,9},{9,8},{10,11... | collective-permute-start | bytes 1032200 | tf_op jit(solution)/shard_map/ppermute | solution.py:188
  413.0 30.4 %collective-permute-start.20 = (bf16[3,224,256]{2,1,0:T(8,128)(2,1)S(1)}, bf16[3,224,256]{2,1,0:T(8,128)(2,1)S(1)}, u32[]{:S(2)}, u32[]{:S(2)}) collective-permute-start(bf16[3,224,256]{2,1,0:T(8,128)(2,1)S(1)} %get-tuple-element.70), channel_id=1, source_target_pairs={{0,3},{1,2},{2,1},{3,0},{4,7},{5,6},{6,5},{7,4},{8,11},{9,10},{10,... | collective-permute-start | bytes 1032200 | tf_op jit(solution)/shard_map/ppermute | solution.py:188
  444.4 293.2 %all-gather.15.cloned.1.call-start = ((), (), s32[]{:S(2)}) async-start(), calls=%async_computation.3 | async-start | bytes 4128768 | tf_op jit(solution)/shard_map/all_gather | solution.py:260
  451.9 16.7 %collective-permute-start.32 = (bf16[896,256]{1,0:T(8,128)(2,1)S(1)}, bf16[896,256]{1,0:T(8,128)(2,1)S(1)}, u32[]{:S(2)}, u32[]{:S(2)}) collective-permute-start(bf16[896,256]{1,0:T(8,128)(2,1)S(1)} %get-tuple-element.65), channel_id=1, source_target_pairs={{0,16},{4,20},{8,24},{12,28},{16,0},{20,4},{24,8},{28,12},{1,17},{... | collective-permute-start | bytes 1376264 | tf_op jit(solution)/shard_map/ppermute | solution.py:195
  452.8 15.9 %collective-permute-start.31 = (bf16[896,256]{1,0:T(8,128)(2,1)S(1)}, bf16[896,256]{1,0:T(8,128)(2,1)S(1)}, u32[]{:S(2)}, u32[]{:S(2)}) collective-permute-start(bf16[896,256]{1,0:T(8,128)(2,1)S(1)} %get-tuple-element.66), channel_id=1, source_target_pairs={{0,8},{4,12},{8,0},{12,4},{16,24},{20,28},{24,16},{28,20},{1,9},{5... | collective-permute-start | bytes 1376264 | tf_op jit(solution)/shard_map/ppermute | solution.py:195
  454.5 14.2 %collective-permute-start.30 = (bf16[896,256]{1,0:T(8,128)(2,1)S(1)}, bf16[896,256]{1,0:T(8,128)(2,1)S(1)}, u32[]{:S(2)}, u32[]{:S(2)}) collective-permute-start(bf16[896,256]{1,0:T(8,128)(2,1)S(1)} %get-tuple-element.62), channel_id=1, source_target_pairs={{0,4},{4,0},{8,12},{12,8},{16,20},{20,16},{24,28},{28,24},{1,5},{5... | collective-permute-start | bytes 1376264 | tf_op jit(solution)/shard_map/ppermute | solution.py:195
  469.1 14.0 %collective-permute-start.34 = (bf16[3,224,256]{2,1,0:T(8,128)(2,1)S(1)}, bf16[3,224,256]{2,1,0:T(8,128)(2,1)S(1)}, u32[]{:S(2)}, u32[]{:S(2)}) collective-permute-start(bf16[3,224,256]{2,1,0:T(8,128)(2,1)S(1)} %get-tuple-element.68), channel_id=1, source_target_pairs={{0,2},{1,3},{2,0},{3,1},{4,6},{5,7},{6,4},{7,5},{8,10},{9,11},{10,... | collective-permute-start | bytes 1032200 | tf_op jit(solution)/shard_map/ppermute | solution.py:188
  469.1 17.5 %collective-permute-start.33 = (bf16[3,224,256]{2,1,0:T(8,128)(2,1)S(1)}, bf16[3,224,256]{2,1,0:T(8,128)(2,1)S(1)}, u32[]{:S(2)}, u32[]{:S(2)}) collective-permute-start(bf16[3,224,256]{2,1,0:T(8,128)(2,1)S(1)} %get-tuple-element.69), channel_id=1, source_target_pairs={{0,1},{1,0},{2,3},{3,2},{4,5},{5,4},{6,7},{7,6},{8,9},{9,8},{10,11... | collective-permute-start | bytes 1032200 | tf_op jit(solution)/shard_map/ppermute | solution.py:188
  472.0 40.0 %collective-permute-start.35 = (bf16[3,224,256]{2,1,0:T(8,128)(2,1)S(1)}, bf16[3,224,256]{2,1,0:T(8,128)(2,1)S(1)}, u32[]{:S(2)}, u32[]{:S(2)}) collective-permute-start(bf16[3,224,256]{2,1,0:T(8,128)(2,1)S(1)} %get-tuple-element.67), channel_id=1, source_target_pairs={{0,3},{1,2},{2,1},{3,0},{4,7},{5,6},{6,5},{7,4},{8,11},{9,10},{10,... | collective-permute-start | bytes 1032200 | tf_op jit(solution)/shard_map/ppermute | solution.py:188
  483.1 49.3 %collective-permute-start.29 = (bf16[224,512]{0,1:T(8,128)(2,1)}, bf16[224,512]{0,1:T(8,128)(2,1)}, u32[]{:S(2)}, u32[]{:S(2)}) collective-permute-start(bf16[224,512]{0,1:T(8,128)(2,1)} %get-tuple-element.74), channel_id=1, source_target_pairs={{0,3},{1,2},{2,1},{3,0},{4,7},{5,6},{6,5},{7,4},{8,11},{9,10},{10,... | collective-permute-start | bytes 688136 | tf_op jit(solution)/shard_map/ppermute | solution.py:188
  486.6 47.3 %collective-permute-start.28 = (bf16[224,512]{0,1:T(8,128)(2,1)}, bf16[224,512]{0,1:T(8,128)(2,1)}, u32[]{:S(2)}, u32[]{:S(2)}) collective-permute-start(bf16[224,512]{0,1:T(8,128)(2,1)} %get-tuple-element.75), channel_id=1, source_target_pairs={{0,2},{1,3},{2,0},{3,1},{4,6},{5,7},{6,4},{7,5},{8,10},{9,11},{10,... | collective-permute-start | bytes 688136 | tf_op jit(solution)/shard_map/ppermute | solution.py:188
  512.0 21.9 %collective-permute-start.27 = (bf16[224,512]{0,1:T(8,128)(2,1)}, bf16[224,512]{0,1:T(8,128)(2,1)}, u32[]{:S(2)}, u32[]{:S(2)}) collective-permute-start(bf16[224,512]{0,1:T(8,128)(2,1)} %get-tuple-element.73), channel_id=1, source_target_pairs={{0,1},{1,0},{2,3},{3,2},{4,5},{5,4},{6,7},{7,6},{8,9},{9,8},{10,11... | collective-permute-start | bytes 688136 | tf_op jit(solution)/shard_map/ppermute | solution.py:188
  532.4 39.6 %collective-permute-start.39 = (bf16[224,256]{1,0:T(8,128)(2,1)S(1)}, bf16[224,256]{1,0:T(8,128)(2,1)S(1)}, u32[]{:S(2)}, u32[]{:S(2)}) collective-permute-start(bf16[224,256]{1,0:T(8,128)(2,1)S(1)} %copy-done.45), channel_id=1, source_target_pairs={{0,1},{1,0},{2,3},{3,2},{4,5},{5,4},{6,7},{7,6},{8,9},{9,8},{10,11... | collective-permute-start | bytes 344072 | tf_op jit(solution)/shard_map/ppermute | solution.py:188
  533.9 40.8 %collective-permute-start.50 = (bf16[224,256]{1,0:T(8,128)(2,1)S(1)}, bf16[224,256]{1,0:T(8,128)(2,1)S(1)}, u32[]{:S(2)}, u32[]{:S(2)}) collective-permute-start(bf16[224,256]{1,0:T(8,128)(2,1)S(1)} %copy-done.44), channel_id=1, source_target_pairs={{0,3},{1,2},{2,1},{3,0},{4,7},{5,6},{6,5},{7,4},{8,11},{9,10},{10,... | collective-permute-start | bytes 344072 | tf_op jit(solution)/shard_map/ppermute | solution.py:188
  533.9 122.7 %collective-permute-start.36 = (bf16[4,6,64,256]{3,2,1,0:T(8,128)(2,1)}, bf16[4,6,64,256]{3,2,1,0:T(8,128)(2,1)}, u32[]{:S(2)}, u32[]{:S(2)}) collective-permute-start(bf16[4,6,64,256]{3,2,1,0:T(8,128)(2,1)} %get-tuple-element.48), channel_id=1, source_target_pairs={{0,1},{1,0},{2,3},{3,2},{4,5},{5,4},{6,7},{7,6},{8,9},{9,8},{10,11... | collective-permute-start | bytes 2359304 | tf_op jit(solution)/shard_map/ppermute | solution.py:188
  569.6 19.6 %collective-permute-start.44 = (bf16[224,512]{0,1:T(8,128)(2,1)S(1)}, bf16[224,512]{0,1:T(8,128)(2,1)S(1)}, u32[]{:S(2)}, u32[]{:S(2)}) collective-permute-start(bf16[224,512]{0,1:T(8,128)(2,1)S(1)} %all-reduce.4), channel_id=1, source_target_pairs={{0,3},{1,2},{2,1},{3,0},{4,7},{5,6},{6,5},{7,4},{8,11},{9,10},{10,... | collective-permute-start | bytes 688136 | tf_op jit(solution)/shard_map/ppermute | solution.py:188
  570.8 42.2 %collective-permute-start.43 = (bf16[224,512]{0,1:T(8,128)(2,1)S(1)}, bf16[224,512]{0,1:T(8,128)(2,1)S(1)}, u32[]{:S(2)}, u32[]{:S(2)}) collective-permute-start(bf16[224,512]{0,1:T(8,128)(2,1)S(1)} %all-reduce.4), channel_id=1, source_target_pairs={{0,2},{1,3},{2,0},{3,1},{4,6},{5,7},{6,4},{7,5},{8,10},{9,11},{10,... | collective-permute-start | bytes 688136 | tf_op jit(solution)/shard_map/ppermute | solution.py:188
  572.0 43.3 %collective-permute-start.42 = (bf16[224,512]{0,1:T(8,128)(2,1)S(1)}, bf16[224,512]{0,1:T(8,128)(2,1)S(1)}, u32[]{:S(2)}, u32[]{:S(2)}) collective-permute-start(bf16[224,512]{0,1:T(8,128)(2,1)S(1)} %all-reduce.4), channel_id=1, source_target_pairs={{0,1},{1,0},{2,3},{3,2},{4,5},{5,4},{6,7},{7,6},{8,9},{9,8},{10,11... | collective-permute-start | bytes 688136 | tf_op jit(solution)/shard_map/ppermute | solution.py:188
  574.7 85.2 %collective-permute-start.37 = (bf16[4,6,64,256]{3,2,1,0:T(8,128)(2,1)S(1)}, bf16[4,6,64,256]{3,2,1,0:T(8,128)(2,1)S(1)}, u32[]{:S(2)}, u32[]{:S(2)}) collective-permute-start(bf16[4,6,64,256]{3,2,1,0:T(8,128)(2,1)S(1)} %copy-done.29), channel_id=1, source_target_pairs={{0,2},{1,3},{2,0},{3,1},{4,6},{5,7},{6,4},{7,5},{8,10},{9,11},{10,... | collective-permute-start | bytes 2359304 | tf_op jit(solution)/shard_map/ppermute | solution.py:188
  579.1 75.6 %copy-start.41 = (bf16[224,256]{1,0:T(8,128)(2,1)S(1)}, bf16[224,256]{1,0:T(8,128)(2,1)}, u32[]{:S(2)}) copy-start(bf16[224,256]{1,0:T(8,128)(2,1)} %get-tuple-element.88) | copy-start | bytes 344068
  580.4 76.5 %copy-start.40 = (bf16[224,256]{1,0:T(8,128)(2,1)S(1)}, bf16[224,256]{1,0:T(8,128)(2,1)}, u32[]{:S(2)}) copy-start(bf16[224,256]{1,0:T(8,128)(2,1)} %get-tuple-element.84) | copy-start | bytes 344068
  589.2 60.1 %collective-permute-start.49 = (bf16[224,256]{1,0:T(8,128)(2,1)S(1)}, bf16[224,256]{1,0:T(8,128)(2,1)S(1)}, u32[]{:S(2)}, u32[]{:S(2)}) collective-permute-start(bf16[224,256]{1,0:T(8,128)(2,1)S(1)} %copy-done.43), channel_id=1, source_target_pairs={{0,2},{1,3},{2,0},{3,1},{4,6},{5,7},{6,4},{7,5},{8,10},{9,11},{10,... | collective-permute-start | bytes 344072 | tf_op jit(solution)/shard_map/ppermute | solution.py:188
  613.1 38.5 %collective-permute-start.48 = (bf16[224,256]{1,0:T(8,128)(2,1)S(1)}, bf16[224,256]{1,0:T(8,128)(2,1)S(1)}, u32[]{:S(2)}, u32[]{:S(2)}) collective-permute-start(bf16[224,256]{1,0:T(8,128)(2,1)S(1)} %copy-done.42), channel_id=1, source_target_pairs={{0,1},{1,0},{2,3},{3,2},{4,5},{5,4},{6,7},{7,6},{8,9},{9,8},{10,11... | collective-permute-start | bytes 344072 | tf_op jit(solution)/shard_map/ppermute | solution.py:188
  615.3 51.9 %collective-permute-start.38 = (bf16[4,6,64,256]{3,2,1,0:T(8,128)(2,1)S(1)}, bf16[4,6,64,256]{3,2,1,0:T(8,128)(2,1)S(1)}, u32[]{:S(2)}, u32[]{:S(2)}) collective-permute-start(bf16[4,6,64,256]{3,2,1,0:T(8,128)(2,1)S(1)} %copy-done.28), channel_id=1, source_target_pairs={{0,3},{1,2},{2,1},{3,0},{4,7},{5,6},{6,5},{7,4},{8,11},{9,10},{10,... | collective-permute-start | bytes 2359304 | tf_op jit(solution)/shard_map/ppermute | solution.py:188
  649.3 21.9 %collective-permute-start.45 = (bf16[4,6,64,256]{3,2,1,0:T(8,128)(2,1)S(1)}, bf16[4,6,64,256]{3,2,1,0:T(8,128)(2,1)S(1)}, u32[]{:S(2)}, u32[]{:S(2)}) collective-permute-start(bf16[4,6,64,256]{3,2,1,0:T(8,128)(2,1)S(1)} %get-tuple-element.44), channel_id=1, source_target_pairs={{0,1},{1,0},{2,3},{3,2},{4,5},{5,4},{6,7},{7,6},{8,9},{9,8},{10,11... | collective-permute-start | bytes 2359304 | tf_op jit(solution)/shard_map/ppermute | solution.py:188
  651.5 65.2 %collective-permute-start.46 = (bf16[4,6,64,256]{3,2,1,0:T(8,128)(2,1)S(1)}, bf16[4,6,64,256]{3,2,1,0:T(8,128)(2,1)S(1)}, u32[]{:S(2)}, u32[]{:S(2)}) collective-permute-start(bf16[4,6,64,256]{3,2,1,0:T(8,128)(2,1)S(1)} %get-tuple-element.43), channel_id=1, source_target_pairs={{0,2},{1,3},{2,0},{3,1},{4,6},{5,7},{6,4},{7,5},{8,10},{9,11},{10,... | collective-permute-start | bytes 2359304 | tf_op jit(solution)/shard_map/ppermute | solution.py:188
  656.7 77.7 %collective-permute-start.47 = (bf16[4,6,64,256]{3,2,1,0:T(8,128)(2,1)S(1)}, bf16[4,6,64,256]{3,2,1,0:T(8,128)(2,1)S(1)}, u32[]{:S(2)}, u32[]{:S(2)}) collective-permute-start(bf16[4,6,64,256]{3,2,1,0:T(8,128)(2,1)S(1)} %get-tuple-element.42), channel_id=1, source_target_pairs={{0,3},{1,2},{2,1},{3,0},{4,7},{5,6},{6,5},{7,4},{8,11},{9,10},{10,... | collective-permute-start | bytes 2359304 | tf_op jit(solution)/shard_map/ppermute | solution.py:188
  671.2 65.3 %copy-start.21 = (bf16[256,1024]{1,0:T(8,128)(2,1)S(1)}, bf16[256,1024]{1,0:T(8,128)(2,1)}, u32[]{:S(2)}) copy-start(bf16[256,1024]{1,0:T(8,128)(2,1)} %copy-done.20) | copy-start | bytes 1572868
  (41 other events, 414.9 us)
Sparse Core Ops, SparseCore 0:
  9.9 36.0 all-gather.8
  47.9 36.6 all-gather.12
  444.5 39.2 all-gather.10
  513.2 37.2 all-gather.14
